TPU v7x, 32 devices: a whole 2x2x4 slice. The times are simulated.
32 devices in a mesh: video: 4 (over x, core), tm: 8 (over z, y).
Axes of the slice: x: 2, y: 2, z: 4, core: 2. Of those that a mesh axis runs over, the one named last changes fastest.
Arguments:
- queries: bfloat16 [4, 8, 4096, 256], P('video', 'tm'), may hold values from -720 to 720
- memory: bfloat16 [4, 8, 64, 4096], P('video', 'tm'), may hold values from -6 to 6
- tpos: float32 [7, 64], replicated, may hold values from -4 to 4
- w_k: bfloat16 [64, 256], replicated, may hold values from -0.75 to 0.75
- w_v: bfloat16 [64, 256], replicated, may hold values from -0.75 to 0.75
- w_o: bfloat16 [256, 256], replicated, may hold values from -0.375 to 0.375
- keyframes: int32 [4, 8, 64], P('video', 'tm'), may hold values from 0 to 511, as said below
- cot: bfloat16 [4, 8, 4096, 256], P('video', 'tm'), may hold values from -6 to 6
Outputs:
- branch: bfloat16 [4, 8, 4096, 256], P('video', 'tm')
- grad_wo: float32 [256, 256], P('tm')
Inputs may be any that keep to these rules, and one draw needn't show every extreme that they name: `keyframes`: each frame's list is made of runs of 16 consecutive entries that lie in one frame; the runs of one list lie in different frames.
All inputs are finite; a program needn't handle non-finite values.
Results may differ from a plain program's by a relative error of at most 0.012.
The roundings to bfloat16 on the way count: a program that leaves them out, or rounds other values in their place, can miss the bound.
Values may be sent and summed in bfloat16 or wider, within the bound.
A program may use at most 128 MiB of HBM per device.

v0:
```python
import functools
import math

import jax
import jax.numpy as jnp
from jax import lax
from jax.experimental import pallas as pl
from jax.experimental.pallas import tpu as pltpu
from jax.sharding import PartitionSpec as P

TT = 64
MD = 64
BACK = 6
CLASSES = 8
PIECES = 8
LOW = -1e30
LANES = 2 * TT
MESH = pl.DeviceIdType.MESH
DIMS_T = (((1,), (1,)), ((), ()))


def ring_pos(me, n):
    return jnp.where(me % 2 == 1, (me + 1) // 2, (n - me // 2) % n)


def ring_at(pos, n):
    return jnp.where((pos >= 1) & (pos <= n // 2), 2 * pos - 1, (2 * (n - pos)) % (2 * n))


def split_tokens(packed, position):
    mixed = (packed.astype(jnp.float32) + position).astype(jnp.bfloat16)
    first = lax.broadcasted_iota(jnp.int32, mixed.shape, mixed.ndim - 1) < MD
    zero = jnp.zeros_like(mixed)
    return jnp.concatenate(
        [jnp.where(first, mixed, zero), jnp.where(first, zero, mixed)], axis=mixed.ndim - 2
    )


def kernel(
    n, videos, norm, keyed_ref, own_ref, q_hbm, cot_hbm, tpos_ref, wk_ref, wv_ref, wo_ref,
    branch_hbm, grad_out,
    frames, q_ref, cot_ref, top_ref, sum_ref, acc_ref, att_ref, branch_ref, wk2, wv2, pos_ref,
    grad_ref, parts, mine, sums,
    local_sem, out_sem, send_r, recv_r, send_l, recv_l, send_a, recv_a, send_b, recv_b,
):
    me = lax.axis_index("tm")
    vid = lax.axis_index("video")
    pos = ring_pos(me, n)
    right = ring_at((pos + 1) % n, n)
    left = ring_at((pos + n - 1) % n, n)
    groups, d = q_ref.shape[0], q_ref.shape[-1]
    tiles = groups * CLASSES
    entries = keyed_ref.shape[0] // CLASSES
    per_piece = groups // PIECES
    far = n // 2
    scale = 1.0 / math.sqrt(d)
    rows = grad_out.shape[0]

    barrier = pltpu.get_barrier_semaphore()
    for step in range(1, n):
        other = (me + step) % n
        pl.semaphore_signal(barrier, inc=1, device_id={"tm": other}, device_id_type=MESH)
    for step in range(1, videos):
        other = (vid + step) % videos
        pl.semaphore_signal(barrier, inc=1, device_id={"video": other}, device_id_type=MESH)
    locals_ = [
        pltpu.make_async_copy(own_ref, frames.at[me], local_sem.at[0]),
        pltpu.make_async_copy(q_hbm, q_ref, local_sem.at[1]),
        pltpu.make_async_copy(cot_hbm, cot_ref, local_sem.at[2]),
    ]
    for copy in locals_:
        copy.start()
    pl.semaphore_wait(barrier, n - 1 + videos - 1)

    def hop(step, piece, rightward):
        origin = ring_at((pos + n - step) % n if rightward else (pos + step) % n, n)
        part = pl.ds(piece * per_piece, per_piece)
        sems = (send_r, recv_r) if rightward else (send_l, recv_l)
        return pltpu.make_async_remote_copy(
            src_ref=own_ref.at[part] if step == 0 else frames.at[origin, part],
            dst_ref=frames.at[origin, part],
            send_sem=sems[0].at[step, piece],
            recv_sem=sems[1].at[step, piece],
            device_id={"tm": right if rightward else left},
            device_id_type=MESH,
        )

    def pieces_of(step):
        if step < far - 1:
            return list(range(PIECES)), list(range(PIECES))
        return list(range(PIECES // 2)), list(range(PIECES // 2, PIECES))

    for pair in zip(*pieces_of(0)):
        hop(0, pair[0], True).start()
        hop(0, pair[1], False).start()

    wk2[...] = jnp.concatenate([wk_ref[...], wk_ref[...]], axis=0)
    wv2[...] = jnp.concatenate([wv_ref[...], wv_ref[...]], axis=0)
    pos_ref[...] = jnp.concatenate([tpos_ref[...], tpos_ref[...]], axis=1)
    top_ref[...] = jnp.full_like(top_ref, LOW)
    sum_ref[...] = jnp.zeros_like(sum_ref)
    acc_ref[...] = jnp.zeros_like(acc_ref)
    locals_[1].wait()
    q_ref[...] = (q_ref[...].astype(jnp.float32) * scale).astype(jnp.bfloat16)

    def keys_of(x):
        return jnp.dot(x, wk2[...], preferred_element_type=jnp.float32).astype(jnp.bfloat16)

    def wide_max(s):
        return jnp.broadcast_to(jnp.max(s, axis=1, keepdims=True), (s.shape[0], LANES))

    def recent(distance, cls):
        origins = [ring_at((pos + n - distance) % n, n)]
        if distance < far:
            origins.append(ring_at((pos + distance) % n, n))
        xs, bias = [], []
        for origin in origins:
            offset = me - origin
            live = (offset >= 1) & (offset <= BACK)
            row = pos_ref[pl.ds(jnp.clip(offset - 1, 0, BACK - 1), 1), :]
            xs.append(split_tokens(frames[origin, :, cls], row[None]))
            bias.append(jnp.full((1, TT), jnp.where(live, 0.0, LOW), jnp.float32))
        x = jnp.concatenate(xs, axis=1)
        width = x.shape[1]
        bias = jnp.concatenate(bias, axis=1)
        keys = keys_of(x.reshape(groups * width, 2 * MD))
        s = jnp.concatenate(
            [
                lax.dot_general(
                    q_ref[g, cls],
                    keys[g * width : (g + 1) * width],
                    DIMS_T,
                    preferred_element_type=jnp.float32,
                )
                for g in range(groups)
            ],
            axis=0,
        )
        s = s + bias
        old = top_ref[cls]
        top = jnp.maximum(old, wide_max(s))
        p = jnp.exp(s - top[:, :width])
        fade = jnp.exp(old - top)
        part = p if width == LANES else jnp.concatenate([p, jnp.zeros_like(p)], axis=1)
        total = sum_ref[cls] * fade + part
        p = p.astype(jnp.bfloat16)
        u = jnp.concatenate(
            [
                jnp.dot(p[g * TT : (g + 1) * TT], x[g], preferred_element_type=jnp.float32)
                for g in range(groups)
            ],
            axis=0,
        )
        acc = acc_ref[cls] * fade + u
        return top, total, acc

    def recent_step(distance, cls):
        top, total, acc = recent(distance, cls)
        top_ref[cls] = top
        sum_ref[cls] = total
        acc_ref[cls] = acc

    for distance in range(1, far + 1):
        pairs = list(zip(*pieces_of(distance - 1)))
        share = CLASSES // len(pairs)
        onward = pieces_of(distance)
        for number, pair in enumerate(pairs):
            for piece, rightward in zip(pair, (True, False)):
                hop(distance - 1, piece, rightward).wait_recv()
                if distance < far and piece in onward[0 if rightward else 1]:
                    hop(distance, piece, rightward).start()
            if distance > 1:

                def some(cls, carry, distance=distance):
                    recent_step(distance - 1, cls)
                    return carry

                lax.fori_loop(number * share, (number + 1) * share, some, 0)
    locals_[0].wait()
    locals_[2].wait()
    grad_ref[...] = jnp.zeros_like(grad_ref)

    def finish(cls, carry):
        top, total, acc = recent(far, cls)
        picked = []
        for s in range(entries):
            k = keyed_ref[cls + CLASSES * s]
            picked.append(frames[k // tiles, (k % tiles) // CLASSES, k % CLASSES])
        xk = split_tokens(jnp.concatenate(picked, axis=0), pos_ref[BACK : BACK + 1, :])
        q = q_ref[:, cls].reshape(groups * TT, d)
        sk = lax.dot_general(q, keys_of(xk), DIMS_T, preferred_element_type=jnp.float32)
        slabs = [sk[:, i : i + LANES] for i in range(0, sk.shape[1], LANES)]
        new = jnp.maximum(top, wide_max(functools.reduce(jnp.maximum, slabs)))
        pk = [jnp.exp(slab - new) for slab in slabs]
        fade = jnp.exp(top - new)
        total = jnp.sum(total * fade + functools.reduce(jnp.add, pk), axis=1, keepdims=True)
        u = acc * fade + jnp.dot(
            jnp.concatenate([p.astype(jnp.bfloat16) for p in pk], axis=1),
            xk,
            preferred_element_type=jnp.float32,
        )
        u = u / total
        attended = jnp.dot(
            u.astype(jnp.bfloat16), wv2[...], preferred_element_type=jnp.float32
        ).astype(jnp.bfloat16)
        att_ref[cls] = attended
        grad_ref[...] += lax.dot_general(
            attended,
            cot_ref[:, cls].reshape(groups * TT, d),
            (((0,), (0,)), ((), ())),
            preferred_element_type=jnp.float32,
        )
        return carry

    lax.fori_loop(0, CLASSES, finish, 0, unroll=2)

    def term(step):
        other = (me + step) % n
        return pltpu.make_async_remote_copy(
            src_ref=grad_ref.at[pl.ds(other * rows, rows)],
            dst_ref=parts.at[step - 1],
            send_sem=send_a.at[step - 1],
            recv_sem=recv_a.at[step - 1],
            device_id={"tm": other},
            device_id_type=MESH,
        )

    def share_of(step):
        other = (vid + step) % videos
        return pltpu.make_async_remote_copy(
            src_ref=mine,
            dst_ref=sums.at[vid],
            send_sem=send_b.at[step - 1],
            recv_sem=recv_b.at[step - 1],
            device_id={"video": other},
            device_id_type=MESH,
        )

    for step in range(1, n):
        term(step).start()

    def put(cls):
        return pltpu.make_async_copy(branch_ref.at[cls], branch_hbm.at[:, cls], out_sem.at[cls])

    def project(cls, carry):
        out = jnp.dot(att_ref[cls], wo_ref[...], preferred_element_type=jnp.float32)
        branch_ref[cls] = out.astype(jnp.bfloat16).reshape(groups, TT, d)
        put(cls).start()
        return carry

    lax.fori_loop(0, CLASSES, project, 0)

    total = grad_ref[pl.ds(pl.multiple_of(me * rows, 8), rows), :]
    for step in range(1, n):
        term(step).wait_recv()
        total = total + parts[step - 1]
    mine[...] = total
    for step in range(1, videos):
        share_of(step).start()
    sums[vid] = total
    for step in range(1, videos):
        share_of(step).wait_recv()
    result = sums[0]
    for other in range(1, videos):
        result = result + sums[other]
    grad_out[...] = result * norm

    for step in range(far):
        rightward, leftward = pieces_of(step)
        for piece in rightward:
            hop(step, piece, True).wait_send()
        for piece in leftward:
            hop(step, piece, False).wait_send()
    for step in range(1, n):
        term(step).wait_send()
    for step in range(1, videos):
        share_of(step).wait_send()
    for cls in range(CLASSES):
        put(cls).wait()


def per_device(n, videos, queries, memory, tpos, w_k, w_v, w_o, keyframes, cot):
    tiles = memory.shape[2]
    d = queries.shape[-1]
    groups = tiles // CLASSES
    grouped = (groups, CLASSES, TT, d)
    own = memory[0, 0].reshape(groups, CLASSES, TT // 2, 2 * MD)
    rows = d // n
    vmem = pl.BlockSpec(memory_space=pltpu.VMEM)
    hbm = pl.BlockSpec(memory_space=pl.ANY)
    dma = pltpu.SemaphoreType.DMA
    f32, bf16 = jnp.float32, jnp.bfloat16
    hops = dma((n // 2, PIECES))
    norm = 1.0 / math.sqrt(videos * n * tiles * TT)
    branch, grad = pl.pallas_call(
        functools.partial(kernel, n, videos, norm),
        out_shape=(
            jax.ShapeDtypeStruct(grouped, bf16),
            jax.ShapeDtypeStruct((rows, d), f32),
        ),
        in_specs=[
            pl.BlockSpec(memory_space=pltpu.SMEM), vmem, hbm, hbm, vmem, vmem, vmem, vmem,
        ],
        out_specs=(hbm, vmem),
        scratch_shapes=[
            pltpu.VMEM((n,) + own.shape, bf16),
            pltpu.VMEM(grouped, bf16),
            pltpu.VMEM(grouped, bf16),
            pltpu.VMEM((CLASSES, groups * TT, LANES), f32),
            pltpu.VMEM((CLASSES, groups * TT, LANES), f32),
            pltpu.VMEM((CLASSES, groups * TT, 2 * MD), f32),
            pltpu.VMEM((CLASSES, groups * TT, d), bf16),
            pltpu.VMEM((CLASSES, groups, TT, d), bf16),
            pltpu.VMEM((2 * MD, d), bf16),
            pltpu.VMEM((2 * MD, d), bf16),
            pltpu.VMEM((BACK + 1, 2 * MD), f32),
            pltpu.VMEM((d, d), f32),
            pltpu.VMEM((n - 1, rows, d), f32),
            pltpu.VMEM((rows, d), f32),
            pltpu.VMEM((videos, rows, d), f32),
            dma((3,)),
            dma((CLASSES,)),
            hops, hops, hops, hops,
            dma((n - 1,)), dma((n - 1,)),
            dma((videos - 1,)), dma((videos - 1,)),
        ],
        compiler_params=pltpu.CompilerParams(
            collective_id=0, has_side_effects=True, vmem_limit_bytes=60 * 1024 * 1024
        ),
        name="attend",
    )(
        keyframes[0, 0], own, queries[0, 0].reshape(grouped), cot[0, 0].reshape(grouped),
        tpos, w_k, w_v, w_o,
    )
    return branch.reshape(queries.shape), grad


def solution(mesh):
    frame_spec = P("video", "tm", None, None)
    in_specs = (frame_spec, frame_spec, P(), P(), P(), P(), P("video", "tm", None), frame_spec)
    out_specs = (frame_spec, P("tm", None))
    return jax.shard_map(
        functools.partial(per_device, mesh.shape["tm"], mesh.shape["video"]),
        mesh=mesh,
        in_specs=in_specs,
        out_specs=out_specs,
        check_vma=False,
    )
```

profile of v0, /device:TPU:0, one launch (start us, length us, event | category | flops | bytes accessed | tf_op | source)
XLA Modules:
  0.0 79.5 jit_solution(8880843508341449939)
XLA Ops:
  0.6 1.9 %copy.12 = bf16[8,8,32,128]{3,2,1,0:T(8,128)(2,1)} copy(bf16[8,8,32,128]{3,1,2,0:T(8,128)(2,1)} %bitcast.14) | data formatting | bytes 1048576
  2.6 73.3 %attend.1 = (bf16[8,8,64,256]{3,2,1,0:T(8,128)(2,1)}, f32[32,256]{1,0:T(8,128)}) custom-call(s32[64]{0:T(128)} %bitcast.15, bf16[8,8,32,128]{3,2,1,0:T(8,128)(2,1)} %copy.12, bf16[8,8,64,256]{3,2,1,0:T(8,128)(2,1)} %bitcast.11, bf16[8,8,64,256]{3,2,1,0:T(8,128)(2,1)} %bitcast.12, f32[7,64]{1,0:T(8,128)} %tpos_ref.1, bf16[64,256]{1,0:T(8,128)(2,1)} %wk_ref.1, ...), custom_call_target="tpu_custom_call" | custom-call | tf_op jit(solution)/shard_map/attend/pallas_call | solution.py:295
  75.9 0.0 copy-start
  75.9 3.0 %copy.15 = bf16[1,1,4096,256]{3,2,1,0:T(8,128)(2,1)} copy(bf16[1,1,4096,256]{3,2,1,0:T(8,128)(2,1)} %bitcast.13) | data formatting | bytes 4194304
  78.9 0.0 copy-done
  78.9 0.6 copy.16
Async XLA Ops:
  75.9 3.1 %copy-start = (f32[32,256]{1,0:T(8,128)S(1)}, f32[32,256]{1,0:T(8,128)}, u32[]{:S(2)}) copy-start(f32[32,256]{1,0:T(8,128)} %get-tuple-element.9) | copy-start | bytes 98308
where the time goes:
time: 79.8 us; the launch traced here: 79.5 us
  Pallas kernels  73.3 us (92%)
  local copies, waits for them, and re-layouts  5.61 us (7%)
    pallas_call x1, Pallas kernels, per_device(): pl.pallas_call(functools.partial(kernel, n, videos, norm), out_shape=(jax...  73.3 us
    unnamed x5, local copies, waits for them, and re-layouts  5.61 us

commit v1 on v0

v1 whole, which is shorter than its diff:
```python
import functools
import math

import jax
import jax.numpy as jnp
from jax import lax
from jax.experimental import pallas as pl
from jax.experimental.pallas import tpu as pltpu
from jax.sharding import PartitionSpec as P

TT = 64
MD = 64
BACK = 6
CLASSES = 8
LOW = -1e30
LANES = 2 * TT
MESH = pl.DeviceIdType.MESH
DIMS_T = (((1,), (1,)), ((), ()))


def ring_pos(me, n):
    return jnp.where(me % 2 == 1, (me + 1) // 2, (n - me // 2) % n)


def ring_at(pos, n):
    return jnp.where((pos >= 1) & (pos <= n // 2), 2 * pos - 1, (2 * (n - pos)) % (2 * n))


def split_tokens(packed, position):
    mixed = (packed.astype(jnp.float32) + position).astype(jnp.bfloat16)
    first = lax.broadcasted_iota(jnp.int32, mixed.shape, mixed.ndim - 1) < MD
    zero = jnp.zeros_like(mixed)
    return jnp.concatenate(
        [jnp.where(first, mixed, zero), jnp.where(first, zero, mixed)], axis=mixed.ndim - 2
    )


def kernel(
    n, videos, norm, keyed_ref, own_hbm, q_hbm, cot_hbm, tpos_ref, wk_ref, wv_ref, wo_ref,
    branch_hbm, grad_out,
    frames, raw_ref, q_ref, cot_ref, top_ref, sum_ref, acc_ref, att_ref, branch_ref, wk2, wv2,
    pos_ref, grad_ref, terms, parts, mine, sums,
    local_sem, out_sem, send_r, recv_r, send_l, recv_l, send_a, recv_a, send_b, recv_b,
):
    me = lax.axis_index("tm")
    vid = lax.axis_index("video")
    pos = ring_pos(me, n)
    right = ring_at((pos + 1) % n, n)
    left = ring_at((pos + n - 1) % n, n)
    groups, d = q_ref.shape[0], q_ref.shape[-1]
    tiles = groups * CLASSES
    entries = keyed_ref.shape[0] // CLASSES
    far = n // 2
    half = groups // 2
    scale = 1.0 / math.sqrt(d)
    rows = grad_out.shape[0]

    barrier = pltpu.get_barrier_semaphore()
    for other in (right, left):
        pl.semaphore_signal(barrier, inc=1, device_id={"tm": other}, device_id_type=MESH)
    for step in range(1, videos):
        other = (vid + step) % videos
        pl.semaphore_signal(barrier, inc=1, device_id={"video": other}, device_id_type=MESH)
    locals_ = [
        pltpu.make_async_copy(own_hbm, raw_ref, local_sem.at[0]),
        pltpu.make_async_copy(q_hbm, q_ref, local_sem.at[1]),
        pltpu.make_async_copy(cot_hbm, cot_ref, local_sem.at[2]),
    ]
    for copy in locals_:
        copy.start()
    locals_[0].wait()

    def arrange(g, carry):
        frames[me, g] = jnp.swapaxes(raw_ref[g], 0, 1)
        return carry

    lax.fori_loop(0, groups, arrange, 0)
    pl.semaphore_wait(barrier, 2 + videos - 1)

    def hop(step, piece, rightward):
        origin = ring_at((pos + n - step) % n if rightward else (pos + step) % n, n)
        sems = (send_r, recv_r) if rightward else (send_l, recv_l)
        return pltpu.make_async_remote_copy(
            src_ref=frames.at[origin, piece],
            dst_ref=frames.at[origin, piece],
            send_sem=sems[0].at[step, piece],
            recv_sem=sems[1].at[step, piece],
            device_id={"tm": right if rightward else left},
            device_id_type=MESH,
        )

    def every(count, body):
        def step(i, carry):
            body(i)
            return carry

        lax.fori_loop(0, count, step, 0)

    def first_hops(g):
        hop(0, g, True).start()
        hop(0, g, False).start()

    every(groups, first_hops)

    wk = (wk_ref[...].astype(jnp.float32) * scale).astype(jnp.bfloat16)
    wk2[...] = jnp.concatenate([wk, wk], axis=0)
    wv2[...] = jnp.concatenate([wv_ref[...], wv_ref[...]], axis=0)
    pos_ref[...] = jnp.concatenate([tpos_ref[...], tpos_ref[...]], axis=1)
    top_ref[...] = jnp.full_like(top_ref, LOW)
    sum_ref[...] = jnp.zeros_like(sum_ref)
    acc_ref[...] = jnp.zeros_like(acc_ref)
    grad_ref[...] = jnp.zeros_like(grad_ref)
    locals_[1].wait()

    def keys_of(x):
        return jnp.dot(x, wk2[...], preferred_element_type=jnp.float32).astype(jnp.bfloat16)

    def wide_max(s):
        return jnp.broadcast_to(jnp.max(s, axis=1, keepdims=True), (s.shape[0], LANES))

    def recent(distance, g):
        origins = [ring_at((pos + n - distance) % n, n)]
        if distance < far:
            origins.append(ring_at((pos + distance) % n, n))
        xs, bias = [], []
        for origin in origins:
            offset = me - origin
            live = (offset >= 1) & (offset <= BACK)
            row = pos_ref[pl.ds(jnp.clip(offset - 1, 0, BACK - 1), 1), :]
            xs.append(split_tokens(frames[origin, g], row[None]))
            bias.append(jnp.full((1, TT), jnp.where(live, 0.0, LOW), jnp.float32))
        x = jnp.concatenate(xs, axis=1)
        width = x.shape[1]
        bias = jnp.concatenate(bias, axis=1)
        keys = keys_of(x.reshape(CLASSES * width, 2 * MD))
        s = jnp.concatenate(
            [
                lax.dot_general(
                    q_ref[g, c],
                    keys[c * width : (c + 1) * width],
                    DIMS_T,
                    preferred_element_type=jnp.float32,
                )
                for c in range(CLASSES)
            ],
            axis=0,
        )
        s = s + bias
        old = top_ref[g].reshape(CLASSES * TT, LANES)
        top = jnp.maximum(old, wide_max(s))
        p = jnp.exp(s - top[:, :width])
        fade = jnp.exp(old - top)
        part = p if width == LANES else jnp.concatenate([p, jnp.zeros_like(p)], axis=1)
        total = sum_ref[g].reshape(CLASSES * TT, LANES) * fade + part
        p = p.astype(jnp.bfloat16)
        u = jnp.concatenate(
            [
                jnp.dot(p[c * TT : (c + 1) * TT], x[c], preferred_element_type=jnp.float32)
                for c in range(CLASSES)
            ],
            axis=0,
        )
        acc = acc_ref[g].reshape(CLASSES * TT, 2 * MD) * fade + u
        top_ref[g] = top.reshape(CLASSES, TT, LANES)
        sum_ref[g] = total.reshape(CLASSES, TT, LANES)
        acc_ref[g] = acc.reshape(CLASSES, TT, 2 * MD)

    for distance in range(1, far):

        def arrive(g, distance=distance):
            for rightward in (True, False):
                hop(distance - 1, g, rightward).wait_recv()
                if distance < far - 1:
                    hop(distance, g, rightward).start()
            if distance == far - 1:
                @pl.when(g < half)
                def _():
                    hop(distance, g, True).start()

                @pl.when(g >= half)
                def _():
                    hop(distance, g, False).start()

            recent(distance, g)

        every(groups, arrive)

    def last(i):
        hop(far - 1, i, True).wait_recv()
        hop(far - 1, half + i, False).wait_recv()
        recent(far, i)
        recent(far, half + i)

    every(half, last)
    locals_[2].wait()

    def finish(cls, carry):
        top = top_ref[:, cls].reshape(groups * TT, LANES)
        picked = []
        for s in range(entries):
            k = keyed_ref[cls + CLASSES * s]
            picked.append(frames[k // tiles, (k % tiles) // CLASSES, k % CLASSES])
        xk = split_tokens(jnp.concatenate(picked, axis=0), pos_ref[BACK : BACK + 1, :])
        q = q_ref[:, cls].reshape(groups * TT, d)
        sk = lax.dot_general(q, keys_of(xk), DIMS_T, preferred_element_type=jnp.float32)
        slabs = [sk[:, i : i + LANES] for i in range(0, sk.shape[1], LANES)]
        new = jnp.maximum(top, wide_max(functools.reduce(jnp.maximum, slabs)))
        pk = [jnp.exp(slab - new) for slab in slabs]
        fade = jnp.exp(top - new)
        total = sum_ref[:, cls].reshape(groups * TT, LANES)
        total = jnp.sum(total * fade + functools.reduce(jnp.add, pk), axis=1, keepdims=True)
        u = acc_ref[:, cls].reshape(groups * TT, 2 * MD) * fade + jnp.dot(
            jnp.concatenate([p.astype(jnp.bfloat16) for p in pk], axis=1),
            xk,
            preferred_element_type=jnp.float32,
        )
        u = u / total
        attended = jnp.dot(
            u.astype(jnp.bfloat16), wv2[...], preferred_element_type=jnp.float32
        ).astype(jnp.bfloat16)
        att_ref[cls] = attended
        grad_ref[...] += lax.dot_general(
            attended,
            cot_ref[:, cls].reshape(groups * TT, d),
            (((0,), (0,)), ((), ())),
            preferred_element_type=jnp.float32,
        )
        return carry

    lax.fori_loop(0, CLASSES, finish, 0, unroll=2)

    def term(step):
        other = (me + step) % n
        return pltpu.make_async_remote_copy(
            src_ref=terms.at[other],
            dst_ref=parts.at[step - 1],
            send_sem=send_a.at[step - 1],
            recv_sem=recv_a.at[step - 1],
            device_id={"tm": other},
            device_id_type=MESH,
        )

    def share_of(step):
        other = (vid + step) % videos
        return pltpu.make_async_remote_copy(
            src_ref=mine,
            dst_ref=sums.at[vid],
            send_sem=send_b.at[step - 1],
            recv_sem=recv_b.at[step - 1],
            device_id={"video": other},
            device_id_type=MESH,
        )

    terms[...] = grad_ref[...].astype(jnp.bfloat16).reshape(terms.shape)
    for step in range(1, n):
        term(step).start()

    def put(cls):
        return pltpu.make_async_copy(branch_ref.at[cls], branch_hbm.at[:, cls], out_sem.at[cls])

    def project(cls, carry):
        out = jnp.dot(att_ref[cls], wo_ref[...], preferred_element_type=jnp.float32)
        branch_ref[cls] = out.astype(jnp.bfloat16).reshape(groups, TT, d)
        put(cls).start()
        return carry

    lax.fori_loop(0, CLASSES, project, 0)

    total = grad_ref[pl.ds(pl.multiple_of(me * rows, 8), rows), :]
    for step in range(1, n):
        term(step).wait_recv()
        total = total + parts[step - 1].astype(jnp.float32)
    mine[...] = total
    for step in range(1, videos):
        share_of(step).start()
    sums[vid] = total
    for step in range(1, videos):
        share_of(step).wait_recv()
    result = sums[0]
    for other in range(1, videos):
        result = result + sums[other]
    grad_out[...] = result * norm

    for step in range(far - 1):

        def sent(g, step=step):
            hop(step, g, True).wait_send()
            hop(step, g, False).wait_send()

        every(groups, sent)

    def last_sent(i):
        hop(far - 1, i, True).wait_send()
        hop(far - 1, half + i, False).wait_send()

    every(half, last_sent)
    for step in range(1, n):
        term(step).wait_send()
    for step in range(1, videos):
        share_of(step).wait_send()
    for cls in range(CLASSES):
        put(cls).wait()


def per_device(n, videos, queries, memory, tpos, w_k, w_v, w_o, keyframes, cot):
    tiles = memory.shape[2]
    d = queries.shape[-1]
    groups = tiles // CLASSES
    grouped = (groups, CLASSES, TT, d)
    packed = (TT // 2, 2 * MD)
    own = jnp.swapaxes(memory[0, 0].reshape((groups, CLASSES) + packed), 1, 2)
    rows = d // n
    vmem = pl.BlockSpec(memory_space=pltpu.VMEM)
    hbm = pl.BlockSpec(memory_space=pl.ANY)
    dma = pltpu.SemaphoreType.DMA
    f32, bf16 = jnp.float32, jnp.bfloat16
    hops = dma((n // 2, groups))
    norm = 1.0 / math.sqrt(videos * n * tiles * TT)
    branch, grad = pl.pallas_call(
        functools.partial(kernel, n, videos, norm),
        out_shape=(
            jax.ShapeDtypeStruct(grouped, bf16),
            jax.ShapeDtypeStruct((rows, d), f32),
        ),
        in_specs=[
            pl.BlockSpec(memory_space=pltpu.SMEM), hbm, hbm, hbm, vmem, vmem, vmem, vmem,
        ],
        out_specs=(hbm, vmem),
        scratch_shapes=[
            pltpu.VMEM((n, groups, CLASSES) + packed, bf16),
            pltpu.VMEM(own.shape, bf16),
            pltpu.VMEM(grouped, bf16),
            pltpu.VMEM(grouped, bf16),
            pltpu.VMEM((groups, CLASSES, TT, LANES), f32),
            pltpu.VMEM((groups, CLASSES, TT, LANES), f32),
            pltpu.VMEM((groups, CLASSES, TT, 2 * MD), f32),
            pltpu.VMEM((CLASSES, groups * TT, d), bf16),
            pltpu.VMEM((CLASSES, groups, TT, d), bf16),
            pltpu.VMEM((2 * MD, d), bf16),
            pltpu.VMEM((2 * MD, d), bf16),
            pltpu.VMEM((BACK + 1, 2 * MD), f32),
            pltpu.VMEM((d, d), f32),
            pltpu.VMEM((n, rows, d), bf16),
            pltpu.VMEM((n - 1, rows, d), bf16),
            pltpu.VMEM((rows, d), f32),
            pltpu.VMEM((videos, rows, d), f32),
            dma((3,)),
            dma((CLASSES,)),
            hops, hops, hops, hops,
            dma((n - 1,)), dma((n - 1,)),
            dma((videos - 1,)), dma((videos - 1,)),
        ],
        compiler_params=pltpu.CompilerParams(
            collective_id=0, has_side_effects=True, vmem_limit_bytes=60 * 1024 * 1024
        ),
        name="attend",
    )(
        keyframes[0, 0], own, queries[0, 0].reshape(grouped), cot[0, 0].reshape(grouped),
        tpos, w_k, w_v, w_o,
    )
    return branch.reshape(queries.shape), grad


def solution(mesh):
    frame_spec = P("video", "tm", None, None)
    in_specs = (frame_spec, frame_spec, P(), P(), P(), P(), P("video", "tm", None), frame_spec)
    out_specs = (frame_spec, P("tm", None))
    return jax.shard_map(
        functools.partial(per_device, mesh.shape["tm"], mesh.shape["video"]),
        mesh=mesh,
        in_specs=in_specs,
        out_specs=out_specs,
        check_vma=False,
    )
```

time: 79.8 us -> 71.6 us (0.90)
  Pallas kernels: 73.3 us -> 67.1 us
  local copies, waits for them, and re-layouts: 5.61 us -> 3.67 us
    pallas_call x1, Pallas kernels: 73.3 us -> 67.1 us  [per_device(): pl.pallas_call(functools.partial(kernel, n, videos, norm), out_shape=(jax...]
    unnamed x5 -> x4, local copies, waits for them, and re-layouts: 5.61 us -> 3.67 us
where the time goes in v1:
time: 71.6 us; the launch traced here: 71.4 us
  Pallas kernels  67.1 us (94%)
  local copies, waits for them, and re-layouts  3.67 us (5%)
    pallas_call x1, Pallas kernels, per_device(): pl.pallas_call(functools.partial(kernel, n, videos, norm), out_shape=(jax...  67.1 us
    unnamed x4, local copies, waits for them, and re-layouts  3.67 us

profile of v1, /device:TPU:0, one launch (start us, length us, event | category | flops | bytes accessed | tf_op | source)
XLA Modules:
  0.0 71.4 jit_solution(5209035944396846751)
XLA Ops:
  0.6 67.1 %attend.1 = (bf16[8,8,64,256]{3,2,1,0:T(8,128)(2,1)}, f32[32,256]{1,0:T(8,128)}) custom-call(s32[64]{0:T(128)} %bitcast.11, bf16[8,32,8,128]{3,2,1,0:T(8,128)(2,1)} %bitcast.10, bf16[8,8,64,256]{3,2,1,0:T(8,128)(2,1)} %bitcast.7, bf16[8,8,64,256]{3,2,1,0:T(8,128)(2,1)} %bitcast.8, f32[7,64]{1,0:T(8,128)} %tpos_ref.1, bf16[64,256]{1,0:T(8,128)(2,1)} %wk_ref.1, ...), custom_call_target="tpu_custom_call" | custom-call | tf_op jit(solution)/shard_map/attend/pallas_call | solution.py:319
  67.7 0.0 copy-start
  67.8 3.0 %copy.12 = bf16[1,1,4096,256]{3,2,1,0:T(8,128)(2,1)} copy(bf16[1,1,4096,256]{3,2,1,0:T(8,128)(2,1)} %bitcast.9) | data formatting | bytes 4194304
  70.8 0.0 copy-done
  70.8 0.6 copy.13
Async XLA Ops:
  67.7 3.1 %copy-start = (f32[32,256]{1,0:T(8,128)S(1)}, f32[32,256]{1,0:T(8,128)}, u32[]{:S(2)}) copy-start(f32[32,256]{1,0:T(8,128)} %get-tuple-element.9) | copy-start | bytes 98308

commit v2 on v1

--- a/solution.py
+++ b/solution.py
@@ -36,10 +36,10 @@
 
 
 def kernel(
-    n, videos, norm, keyed_ref, own_hbm, q_hbm, cot_hbm, tpos_ref, wk_ref, wv_ref, wo_ref,
+    n, videos, norm, keyed_hbm, own_hbm, q_hbm, cot_hbm, tpos_hbm, wk_hbm, wv_hbm, wo_hbm,
     branch_hbm, grad_out,
-    frames, raw_ref, q_ref, cot_ref, top_ref, sum_ref, acc_ref, att_ref, branch_ref, wk2, wv2,
-    pos_ref, grad_ref, terms, parts, mine, sums,
+    frames, keyed_ref, tpos_ref, wk_ref, wv_ref, wo_ref, raw_ref, q_ref, cot_ref, top_ref, sum_ref, acc_ref, mean_ref, branch_ref, wk2, wv2,
+    pos_ref, outer_ref, grad_ref, terms, parts, mine, sums,
     local_sem, out_sem, send_r, recv_r, send_l, recv_l, send_a, recv_a, send_b, recv_b,
 ):
     me = lax.axis_index("tm")
@@ -64,7 +64,12 @@
     locals_ = [
         pltpu.make_async_copy(own_hbm, raw_ref, local_sem.at[0]),
         pltpu.make_async_copy(q_hbm, q_ref, local_sem.at[1]),
-        pltpu.make_async_copy(cot_hbm, cot_ref, local_sem.at[2]),
+        pltpu.make_async_copy(keyed_hbm, keyed_ref, local_sem.at[2]),
+        pltpu.make_async_copy(tpos_hbm, tpos_ref, local_sem.at[3]),
+        pltpu.make_async_copy(wk_hbm, wk_ref, local_sem.at[4]),
+        pltpu.make_async_copy(wv_hbm, wv_ref, local_sem.at[5]),
+        pltpu.make_async_copy(wo_hbm, wo_ref, local_sem.at[6]),
+        pltpu.make_async_copy(cot_hbm, cot_ref, local_sem.at[7]),
     ]
     for copy in locals_:
         copy.start()
@@ -102,6 +107,8 @@
 
     every(groups, first_hops)
 
+    for copy in locals_[2:7]:
+        copy.wait()
     wk = (wk_ref[...].astype(jnp.float32) * scale).astype(jnp.bfloat16)
     wk2[...] = jnp.concatenate([wk, wk], axis=0)
     wv2[...] = jnp.concatenate([wv_ref[...], wv_ref[...]], axis=0)
@@ -109,7 +116,7 @@
     top_ref[...] = jnp.full_like(top_ref, LOW)
     sum_ref[...] = jnp.zeros_like(sum_ref)
     acc_ref[...] = jnp.zeros_like(acc_ref)
-    grad_ref[...] = jnp.zeros_like(grad_ref)
+    outer_ref[...] = jnp.zeros_like(outer_ref)
     locals_[1].wait()
 
     def keys_of(x):
@@ -192,7 +199,7 @@
         recent(far, half + i)
 
     every(half, last)
-    locals_[2].wait()
+    locals_[7].wait()
 
     def finish(cls, carry):
         top = top_ref[:, cls].reshape(groups * TT, LANES)
@@ -214,20 +221,17 @@
             xk,
             preferred_element_type=jnp.float32,
         )
-        u = u / total
-        attended = jnp.dot(
-            u.astype(jnp.bfloat16), wv2[...], preferred_element_type=jnp.float32
-        ).astype(jnp.bfloat16)
-        att_ref[cls] = attended
-        grad_ref[...] += lax.dot_general(
-            attended,
+        u = (u / total).astype(jnp.bfloat16)
+        mean_ref[cls] = u
+        outer_ref[...] += lax.dot_general(
+            u,
             cot_ref[:, cls].reshape(groups * TT, d),
             (((0,), (0,)), ((), ())),
             preferred_element_type=jnp.float32,
         )
         return carry
 
-    lax.fori_loop(0, CLASSES, finish, 0, unroll=2)
+    lax.fori_loop(0, CLASSES, finish, 0, unroll=CLASSES)
 
     def term(step):
         other = (me + step) % n
@@ -251,6 +255,15 @@
             device_id_type=MESH,
         )
 
+    outer = outer_ref[:MD] + outer_ref[MD:]
+    high = outer.astype(jnp.bfloat16)
+    low = (outer - high.astype(jnp.float32)).astype(jnp.bfloat16)
+    grad_ref[...] = sum(
+        lax.dot_general(
+            wv_ref[...], half_, (((0,), (0,)), ((), ())), preferred_element_type=jnp.float32
+        )
+        for half_ in (high, low)
+    )
     terms[...] = grad_ref[...].astype(jnp.bfloat16).reshape(terms.shape)
     for step in range(1, n):
         term(step).start()
@@ -259,7 +272,10 @@
         return pltpu.make_async_copy(branch_ref.at[cls], branch_hbm.at[:, cls], out_sem.at[cls])
 
     def project(cls, carry):
-        out = jnp.dot(att_ref[cls], wo_ref[...], preferred_element_type=jnp.float32)
+        attended = jnp.dot(mean_ref[cls], wv2[...], preferred_element_type=jnp.float32)
+        out = jnp.dot(
+            attended.astype(jnp.bfloat16), wo_ref[...], preferred_element_type=jnp.float32
+        )
         branch_ref[cls] = out.astype(jnp.bfloat16).reshape(groups, TT, d)
         put(cls).start()
         return carry
@@ -323,28 +339,34 @@
             jax.ShapeDtypeStruct((rows, d), f32),
         ),
         in_specs=[
-            pl.BlockSpec(memory_space=pltpu.SMEM), hbm, hbm, hbm, vmem, vmem, vmem, vmem,
+            hbm, hbm, hbm, hbm, hbm, hbm, hbm, hbm,
         ],
         out_specs=(hbm, vmem),
         scratch_shapes=[
             pltpu.VMEM((n, groups, CLASSES) + packed, bf16),
+            pltpu.SMEM(keyframes.shape[2:], jnp.int32),
+            pltpu.VMEM(tpos.shape, f32),
+            pltpu.VMEM(w_k.shape, bf16),
+            pltpu.VMEM(w_v.shape, bf16),
+            pltpu.VMEM(w_o.shape, bf16),
             pltpu.VMEM(own.shape, bf16),
             pltpu.VMEM(grouped, bf16),
             pltpu.VMEM(grouped, bf16),
             pltpu.VMEM((groups, CLASSES, TT, LANES), f32),
             pltpu.VMEM((groups, CLASSES, TT, LANES), f32),
             pltpu.VMEM((groups, CLASSES, TT, 2 * MD), f32),
-            pltpu.VMEM((CLASSES, groups * TT, d), bf16),
+            pltpu.VMEM((CLASSES, groups * TT, 2 * MD), bf16),
             pltpu.VMEM((CLASSES, groups, TT, d), bf16),
             pltpu.VMEM((2 * MD, d), bf16),
             pltpu.VMEM((2 * MD, d), bf16),
             pltpu.VMEM((BACK + 1, 2 * MD), f32),
+            pltpu.VMEM((2 * MD, d), f32),
             pltpu.VMEM((d, d), f32),
             pltpu.VMEM((n, rows, d), bf16),
             pltpu.VMEM((n - 1, rows, d), bf16),
             pltpu.VMEM((rows, d), f32),
             pltpu.VMEM((videos, rows, d), f32),
-            dma((3,)),
+            dma((8,)),
             dma((CLASSES,)),
             hops, hops, hops, hops,
             dma((n - 1,)), dma((n - 1,)),

time: 71.6 us -> 68.6 us (0.958)
  Pallas kernels: 67.1 us -> 64.1 us
    pallas_call x1, Pallas kernels: 67.1 us -> 64.1 us  [per_device(): pl.pallas_call(functools.partial(kernel, n, videos, norm), out_shape=(jax...]
where the time goes in v2:
time: 68.6 us; the launch traced here: 68.4 us
  Pallas kernels  64.1 us (93%)
  local copies, waits for them, and re-layouts  3.67 us (5%)
    pallas_call x1, Pallas kernels, per_device(): pl.pallas_call(functools.partial(kernel, n, videos, norm), out_shape=(jax...  64.1 us
    unnamed x4, local copies, waits for them, and re-layouts  3.67 us

profile of v2, /device:TPU:0, one launch (start us, length us, event | category | flops | bytes accessed | tf_op | source)
XLA Modules:
  0.0 68.4 jit_solution(972898504664362602)
XLA Ops:
  0.6 64.1 %attend.1 = (bf16[8,8,64,256]{3,2,1,0:T(8,128)(2,1)}, f32[32,256]{1,0:T(8,128)}) custom-call(s32[64]{0:T(128)} %bitcast.11, bf16[8,32,8,128]{3,2,1,0:T(8,128)(2,1)} %bitcast.10, bf16[8,8,64,256]{3,2,1,0:T(8,128)(2,1)} %bitcast.7, bf16[8,8,64,256]{3,2,1,0:T(8,128)(2,1)} %bitcast.8, f32[7,64]{1,0:T(8,128)} %tpos_hbm.1, bf16[64,256]{1,0:T(8,128)(2,1)} %wk_hbm.1, ...), custom_call_target="tpu_custom_call" | custom-call | tf_op jit(solution)/shard_map/attend/pallas_call | solution.py:335
  64.8 0.0 copy-start
  64.8 3.0 %copy.12 = bf16[1,1,4096,256]{3,2,1,0:T(8,128)(2,1)} copy(bf16[1,1,4096,256]{3,2,1,0:T(8,128)(2,1)} %bitcast.9) | data formatting | bytes 4194304
  67.8 0.0 copy-done
  67.8 0.6 copy.13
Async XLA Ops:
  64.8 3.1 %copy-start = (f32[32,256]{1,0:T(8,128)S(1)}, f32[32,256]{1,0:T(8,128)}, u32[]{:S(2)}) copy-start(f32[32,256]{1,0:T(8,128)} %get-tuple-element.9) | copy-start | bytes 98308

commit v3 on v2

--- a/solution.py
+++ b/solution.py
@@ -37,10 +37,10 @@
 
 def kernel(
     n, videos, norm, keyed_hbm, own_hbm, q_hbm, cot_hbm, tpos_hbm, wk_hbm, wv_hbm, wo_hbm,
-    branch_hbm, grad_out,
-    frames, keyed_ref, tpos_ref, wk_ref, wv_ref, wo_ref, raw_ref, q_ref, cot_ref, top_ref, sum_ref, acc_ref, mean_ref, branch_ref, wk2, wv2,
+    branch_out, grad_out,
+    frames, keyed_ref, tpos_ref, wk_ref, wv_ref, wo_ref, raw_ref, q_ref, cot_ref, top_ref, sum_ref, acc_ref, mean_ref, wk2, wv2,
     pos_ref, outer_ref, grad_ref, terms, parts, mine, sums,
-    local_sem, out_sem, send_r, recv_r, send_l, recv_l, send_a, recv_a, send_b, recv_b,
+    local_sem, send_r, recv_r, send_l, recv_l, send_a, recv_a, send_b, recv_b,
 ):
     me = lax.axis_index("tm")
     vid = lax.axis_index("video")
@@ -268,16 +268,12 @@
     for step in range(1, n):
         term(step).start()
 
-    def put(cls):
-        return pltpu.make_async_copy(branch_ref.at[cls], branch_hbm.at[:, cls], out_sem.at[cls])
-
     def project(cls, carry):
         attended = jnp.dot(mean_ref[cls], wv2[...], preferred_element_type=jnp.float32)
         out = jnp.dot(
             attended.astype(jnp.bfloat16), wo_ref[...], preferred_element_type=jnp.float32
         )
-        branch_ref[cls] = out.astype(jnp.bfloat16).reshape(groups, TT, d)
-        put(cls).start()
+        branch_out[:, cls] = out.astype(jnp.bfloat16).reshape(groups, TT, d)
         return carry
 
     lax.fori_loop(0, CLASSES, project, 0)
@@ -314,8 +310,6 @@
         term(step).wait_send()
     for step in range(1, videos):
         share_of(step).wait_send()
-    for cls in range(CLASSES):
-        put(cls).wait()
 
 
 def per_device(n, videos, queries, memory, tpos, w_k, w_v, w_o, keyframes, cot):
@@ -335,13 +329,13 @@
     branch, grad = pl.pallas_call(
         functools.partial(kernel, n, videos, norm),
         out_shape=(
-            jax.ShapeDtypeStruct(grouped, bf16),
-            jax.ShapeDtypeStruct((rows, d), f32),
+            pltpu.VMEM(grouped, bf16),
+            pltpu.VMEM((rows, d), f32),
         ),
         in_specs=[
             hbm, hbm, hbm, hbm, hbm, hbm, hbm, hbm,
         ],
-        out_specs=(hbm, vmem),
+        out_specs=(vmem, vmem),
         scratch_shapes=[
             pltpu.VMEM((n, groups, CLASSES) + packed, bf16),
             pltpu.SMEM(keyframes.shape[2:], jnp.int32),
@@ -356,7 +350,6 @@
             pltpu.VMEM((groups, CLASSES, TT, LANES), f32),
             pltpu.VMEM((groups, CLASSES, TT, 2 * MD), f32),
             pltpu.VMEM((CLASSES, groups * TT, 2 * MD), bf16),
-            pltpu.VMEM((CLASSES, groups, TT, d), bf16),
             pltpu.VMEM((2 * MD, d), bf16),
             pltpu.VMEM((2 * MD, d), bf16),
             pltpu.VMEM((BACK + 1, 2 * MD), f32),
@@ -367,13 +360,12 @@
             pltpu.VMEM((rows, d), f32),
             pltpu.VMEM((videos, rows, d), f32),
             dma((8,)),
-            dma((CLASSES,)),
             hops, hops, hops, hops,
             dma((n - 1,)), dma((n - 1,)),
             dma((videos - 1,)), dma((videos - 1,)),
         ],
         compiler_params=pltpu.CompilerParams(
-            collective_id=0, has_side_effects=True, vmem_limit_bytes=60 * 1024 * 1024
+            collective_id=0, has_side_effects=True, vmem_limit_bytes=58 * 1024 * 1024
         ),
         name="attend",
     )(

time: 68.6 us -> 66.2 us (0.965)
  local copies, waits for them, and re-layouts: 3.67 us -> 1.94 us
  Pallas kernels: 64.1 us -> 63.4 us
    unnamed x4 -> x2, local copies, waits for them, and re-layouts: 3.67 us -> 1.94 us
    pallas_call x1, Pallas kernels: 64.1 us -> 63.4 us  [per_device(): pl.pallas_call(functools.partial(kernel, n, videos, norm), out_shape=(plt...]
where the time goes in v3:
time: 66.2 us; the launch traced here: 66 us
  Pallas kernels  63.4 us (96%)
  local copies, waits for them, and re-layouts  1.94 us (3%)
    pallas_call x1, Pallas kernels, per_device(): pl.pallas_call(functools.partial(kernel, n, videos, norm), out_shape=(plt...  63.4 us
    unnamed x2, local copies, waits for them, and re-layouts  1.94 us

profile of v3, /device:TPU:0, one launch (start us, length us, event | category | flops | bytes accessed | tf_op | source)
XLA Modules:
  0.0 66.0 jit_solution(9557505103240105746)
XLA Ops:
  0.6 63.4 %attend.1 = (bf16[8,8,64,256]{3,2,1,0:T(8,128)(2,1)S(1)}, f32[32,256]{1,0:T(8,128)S(1)}) custom-call(s32[64]{0:T(128)} %bitcast.11, bf16[8,32,8,128]{3,2,1,0:T(8,128)(2,1)} %bitcast.10, bf16[8,8,64,256]{3,2,1,0:T(8,128)(2,1)} %bitcast.8, bf16[8,8,64,256]{3,2,1,0:T(8,128)(2,1)} %bitcast.9, f32[7,64]{1,0:T(8,128)} %tpos_hbm.1, bf16[64,256]{1,0:T(8,128)(2,1)} %wk_hbm.1, ...), custom_call_target="tpu_custom_call" | custom-call | tf_op jit(solution)/shard_map/attend/pallas_call | solution.py:329
  64.1 1.3 %copy.12 = bf16[1,1,4096,256]{3,2,1,0:T(8,128)(2,1)} copy(bf16[1,1,4096,256]{3,2,1,0:T(8,128)(2,1)S(1)} %bitcast.7) | data formatting | bytes 4194304
  65.4 0.6 copy.13

commit v4 on v3

--- a/solution.py
+++ b/solution.py
@@ -282,15 +282,16 @@
     for step in range(1, n):
         term(step).wait_recv()
         total = total + parts[step - 1].astype(jnp.float32)
+    total = total.astype(jnp.bfloat16)
     mine[...] = total
     for step in range(1, videos):
         share_of(step).start()
     sums[vid] = total
     for step in range(1, videos):
         share_of(step).wait_recv()
-    result = sums[0]
+    result = sums[0].astype(jnp.float32)
     for other in range(1, videos):
-        result = result + sums[other]
+        result = result + sums[other].astype(jnp.float32)
     grad_out[...] = result * norm
 
     for step in range(far - 1):
@@ -357,8 +358,8 @@
             pltpu.VMEM((d, d), f32),
             pltpu.VMEM((n, rows, d), bf16),
             pltpu.VMEM((n - 1, rows, d), bf16),
-            pltpu.VMEM((rows, d), f32),
-            pltpu.VMEM((videos, rows, d), f32),
+            pltpu.VMEM((rows, d), bf16),
+            pltpu.VMEM((videos, rows, d), bf16),
             dma((8,)),
             hops, hops, hops, hops,
             dma((n - 1,)), dma((n - 1,)),

time: 66.2 us -> 66 us (level)
  no operation moved by 1% of the time
where the time goes in v4:
time: 66 us; the launch traced here: 65.8 us
  Pallas kernels  63.3 us (96%)
  local copies, waits for them, and re-layouts  1.94 us (3%)
    pallas_call x1, Pallas kernels, per_device(): pl.pallas_call(functools.partial(kernel, n, videos, norm), out_shape=(plt...  63.3 us
    unnamed x2, local copies, waits for them, and re-layouts  1.94 us

profile of v4, /device:TPU:0, one launch (start us, length us, event | category | flops | bytes accessed | tf_op | source)
XLA Modules:
  0.0 65.8 jit_solution(13909473813302092830)
XLA Ops:
  0.6 63.3 %attend.1 = (bf16[8,8,64,256]{3,2,1,0:T(8,128)(2,1)S(1)}, f32[32,256]{1,0:T(8,128)S(1)}) custom-call(s32[64]{0:T(128)} %bitcast.11, bf16[8,32,8,128]{3,2,1,0:T(8,128)(2,1)} %bitcast.10, bf16[8,8,64,256]{3,2,1,0:T(8,128)(2,1)} %bitcast.8, bf16[8,8,64,256]{3,2,1,0:T(8,128)(2,1)} %bitcast.9, f32[7,64]{1,0:T(8,128)} %tpos_hbm.1, bf16[64,256]{1,0:T(8,128)(2,1)} %wk_hbm.1, ...), custom_call_target="tpu_custom_call" | custom-call | tf_op jit(solution)/shard_map/attend/pallas_call | solution.py:330
  63.9 1.3 %copy.12 = bf16[1,1,4096,256]{3,2,1,0:T(8,128)(2,1)} copy(bf16[1,1,4096,256]{3,2,1,0:T(8,128)(2,1)S(1)} %bitcast.7) | data formatting | bytes 4194304
  65.2 0.6 copy.13

commit v5 on v3

--- a/solution.py
+++ b/solution.py
@@ -198,7 +198,8 @@
         recent(far, i)
         recent(far, half + i)
 
-    every(half, last)
+    for i in range(half):
+        last(i)
     locals_[7].wait()
 
     def finish(cls, carry):

time: 66.2 us -> 66.1 us (level)
  no operation moved by 1% of the time
where the time goes in v5:
time: 66.1 us; the launch traced here: 66 us
  Pallas kernels  63.4 us (96%)
  local copies, waits for them, and re-layouts  1.94 us (3%)
    pallas_call x1, Pallas kernels, per_device(): pl.pallas_call(functools.partial(kernel, n, videos, norm), out_shape=(plt...  63.4 us
    unnamed x2, local copies, waits for them, and re-layouts  1.94 us

profile of v5, /device:TPU:0, one launch (start us, length us, event | category | flops | bytes accessed | tf_op | source)
XLA Modules:
  0.0 66.0 jit_solution(48311824223606939)
XLA Ops:
  0.6 63.4 %attend.1 = (bf16[8,8,64,256]{3,2,1,0:T(8,128)(2,1)S(1)}, f32[32,256]{1,0:T(8,128)S(1)}) custom-call(s32[64]{0:T(128)} %bitcast.11, bf16[8,32,8,128]{3,2,1,0:T(8,128)(2,1)} %bitcast.10, bf16[8,8,64,256]{3,2,1,0:T(8,128)(2,1)} %bitcast.8, bf16[8,8,64,256]{3,2,1,0:T(8,128)(2,1)} %bitcast.9, f32[7,64]{1,0:T(8,128)} %tpos_hbm.1, bf16[64,256]{1,0:T(8,128)(2,1)} %wk_hbm.1, ...), custom_call_target="tpu_custom_call" | custom-call | tf_op jit(solution)/shard_map/attend/pallas_call | solution.py:330
  64.1 1.3 %copy.12 = bf16[1,1,4096,256]{3,2,1,0:T(8,128)(2,1)} copy(bf16[1,1,4096,256]{3,2,1,0:T(8,128)(2,1)S(1)} %bitcast.7) | data formatting | bytes 4194304
  65.4 0.6 copy.13
